TPU v7x, 256 devices: a whole 4x4x8 slice. The times are simulated.
256 devices in a mesh: req: 4 (over y), blk: 16 (over z, x_lo), tp: 4 (over x_hi, core).
Axes of the slice: x: 4 (x_hi: 2, x_lo: 2; x = x_hi * 2 + x_lo), y: 4, z: 8, core: 2. Of those that a mesh axis runs over, the one named last changes fastest.
Arguments:
- tokens: bfloat16 [4, 2048, 5120], P('req', 'blk', 'tp'), may hold values from -6 to 6
- gain: bfloat16 [5120], replicated, may hold values from 0.5 to 1.5
- w_query: bfloat16 [5120, 5120], P('req', 'tp'), may hold values from -0.078125 to 0.078125
- b_query: bfloat16 [5120], P('tp'), may hold values from -4 to 4
- w_keyval: bfloat16 [5120, 2, 1024], P('req', None, 'tp'), may hold values from -0.078125 to 0.078125
- b_keyval: bfloat16 [2, 1024], P(None, 'tp'), may hold values from -3 to 3
- kv_cache: bfloat16 [4, 2, 112, 128, 1024], P('req', None, 'blk', None, 'tp'), may hold values from -400 to 400
- cached_pages: int32 [4], P('req'), may hold values from 1 to 64, as said below
- page_table: int32 [4, 80], P('req'), may hold values from -1 to 111, as said below
Outputs:
- attended: bfloat16 [4, 2048, 5120], P('req', 'blk', 'tp')
- new_cache: bfloat16 [4, 2, 112, 128, 1024], P('req', None, 'blk', None, 'tp')
Inputs may be any that keep to these rules, and one draw needn't show every extreme that they name: `cached_pages`: one request has the most, 64. `page_table`: entry p of a request's row is the slot (owner index of blk times 7 plus slot) of its logical page p for p below its cached pages plus 16, and -1 beyond; the live pages of a request use distinct slots; one index of blk holds at most 4 cached pages of a request; the request with 64 cached pages has exactly 4 on every index of blk.
All inputs are finite; a program needn't handle non-finite values.
Results may differ from a plain program's by a relative error of at most 0.012.
The roundings to bfloat16 on the way count: a program that leaves them out, or rounds other values in their place, can miss the bound.
Values may be sent and summed in bfloat16 or wider, within the bound.
A program may use at most 128 MiB of HBM per device.

v0:
```python
import jax
import jax.numpy as jnp
from jax import lax
from jax.sharding import PartitionSpec as P

HEAD_SIZE = 128
PAGE_TOKENS = 128
epsilon = 1e-06
rope_base = 1000000.0


def normalize(inputs, gain):
    floats = inputs.astype(jnp.float32)
    scaling = lax.rsqrt(jnp.mean(floats * floats, axis=-1, keepdims=True) + epsilon)
    return (floats * scaling * gain.astype(jnp.float32)).astype(jnp.bfloat16)


def apply_rotation(vectors, token_positions):
    halfway = vectors.shape[-1] // 2
    frequency = rope_base ** (-(jnp.arange(halfway, dtype=jnp.float32) * 2.0 / vectors.shape[-1]))
    angles = token_positions[:, None] * frequency[None, :]
    cosine = jnp.cos(angles)[:, None, :]
    sine_part = jnp.sin(angles)[:, None, :]
    leading = vectors[..., :halfway]
    trailing = vectors[..., halfway:]
    return jnp.concatenate(
        [leading * cosine - trailing * sine_part, trailing * cosine + leading * sine_part], axis=-1
    )


def attend(running, query_rows_all, key_rows, value_rows, allowed):
    scaling = HEAD_SIZE ** (-0.5)
    scores = (
        jnp.einsum("rgjd,kgd->rgjk", query_rows_all, key_rows, preferred_element_type=jnp.float32)
        * scaling
    )
    scores = jnp.where(allowed[:, None, None, :], scores, -jnp.inf)
    maxima, totals, blended = running
    fresh_max = jnp.maximum(maxima, jnp.max(scores, axis=-1))
    weights = jnp.exp(scores - fresh_max[..., None])
    decays = jnp.exp(maxima - fresh_max)
    totals = totals * decays + jnp.sum(weights, axis=-1)
    blended = blended * decays[..., None] + jnp.einsum(
        "rgjk,kgd->rgjd",
        weights.astype(jnp.bfloat16),
        value_rows,
        preferred_element_type=jnp.float32,
    )
    return (fresh_max, totals, blended)


def make_fold(usable_all, query_rows_all, kv_heads_local, running, pieces):
    count = pieces.shape[1]
    stride = max((divisor for divisor in (4, 3, 2, 1) if count % divisor == 0))

    def advance(counter, carried):
        segment = lax.dynamic_slice_in_dim(pieces, counter * stride, stride, 1)
        usable = lax.dynamic_slice_in_dim(usable_all, counter * stride, stride)
        key_rows = segment[0].reshape(stride * PAGE_TOKENS, kv_heads_local, HEAD_SIZE)
        value_rows = segment[1].reshape(stride * PAGE_TOKENS, kv_heads_local, HEAD_SIZE)
        allowed = jnp.repeat(usable, PAGE_TOKENS)[None, :]
        return attend(carried, query_rows_all, key_rows, value_rows, allowed)

    return lax.fori_loop(0, count // stride, advance, running)


def body(tokens, gain, w_query, b_query, w_keyval, b_keyval, kv_cache, cached_pages, page_table):
    whole = lax.all_gather(tokens[0], "tp", axis=1, tiled=True)
    normed = normalize(whole, gain)
    rows_here = normed.shape[0]
    query_width = w_query.shape[1]
    kv_width = w_keyval.shape[2]
    pair_width = 2 * kv_width
    pieces = (
        lax.all_gather(w_query, "req", axis=0, tiled=True),
        lax.all_gather(w_keyval, "req", axis=0, tiled=True),
    )
    count = pieces[0].shape[0]
    query_sum = jnp.dot(normed, pieces[0], preferred_element_type=jnp.float32)
    pair_sum = jnp.dot(
        normed, pieces[1].reshape(count, pair_width), preferred_element_type=jnp.float32
    )
    length = cached_pages[0]
    page_map = page_table[0]
    own_index = lax.axis_index("blk")
    cycle_size = lax.axis_size("blk")
    heads_local = query_width // HEAD_SIZE
    kv_heads_local = kv_width // HEAD_SIZE
    queries_per_group = heads_local // kv_heads_local
    token_index = own_index * rows_here + jnp.arange(rows_here, dtype=jnp.int32)
    token_positions = (length * PAGE_TOKENS + token_index).astype(jnp.float32)
    query_full = query_sum + b_query.astype(jnp.float32)
    query_rows_all = apply_rotation(
        query_full.reshape(rows_here, heads_local, HEAD_SIZE), token_positions
    ).astype(jnp.bfloat16)
    query_rows_all = query_rows_all.reshape(rows_here, kv_heads_local, queries_per_group, HEAD_SIZE)
    pair_full = pair_sum + b_keyval.reshape(pair_width).astype(jnp.float32)
    fresh_key = apply_rotation(
        pair_full[:, :kv_width].reshape(rows_here, kv_heads_local, HEAD_SIZE), token_positions
    ).astype(jnp.bfloat16)
    fresh_value = pair_full[:, kv_width:].astype(jnp.bfloat16)
    fresh_pages = jnp.stack([fresh_key.reshape(rows_here, kv_width), fresh_value]).reshape(
        2, rows_here // PAGE_TOKENS, PAGE_TOKENS, kv_width
    )
    every_page = lax.all_gather(fresh_pages, "blk", axis=1, tiled=True)
    new_count = every_page.shape[1]
    fresh_rows = new_count * PAGE_TOKENS
    new_keys = every_page[0].reshape(fresh_rows, kv_heads_local, HEAD_SIZE)
    new_values = every_page[1].reshape(fresh_rows, kv_heads_local, HEAD_SIZE)
    allowed_fresh = jnp.arange(fresh_rows, dtype=jnp.int32)[None, :] <= token_index[:, None]
    starting = (
        jnp.full((rows_here, kv_heads_local, queries_per_group), -jnp.inf, jnp.float32),
        jnp.zeros((rows_here, kv_heads_local, queries_per_group), jnp.float32),
        jnp.zeros((rows_here, kv_heads_local, queries_per_group, HEAD_SIZE), jnp.float32),
    )
    running = attend(starting, query_rows_all, new_keys, new_values, allowed_fresh)
    cache_storage = kv_cache[0]
    slot_count = cache_storage.shape[1]
    new_slots = lax.dynamic_slice_in_dim(page_map, length, new_count)
    chooser = (
        new_slots[None, :]
        == own_index * slot_count + jnp.arange(slot_count, dtype=jnp.int32)[:, None]
    )
    written = jnp.einsum(
        "sj,cjpw->cspw",
        chooser.astype(jnp.bfloat16),
        every_page,
        preferred_element_type=jnp.float32,
    ).astype(jnp.bfloat16)
    landed = jnp.any(chooser, axis=1)
    new_storage = jnp.where(landed[None, :, None, None], written, cache_storage)
    pool_size = cycle_size * slot_count
    live = jnp.arange(page_map.shape[0], dtype=jnp.int32) < length
    matches = (page_map[None, :] == jnp.arange(pool_size, dtype=jnp.int32)[:, None]) & live[None, :]
    valid = jnp.any(matches, axis=1)
    running = make_fold(
        valid,
        query_rows_all,
        kv_heads_local,
        running,
        lax.all_gather(cache_storage, "blk", axis=1, tiled=True),
    )
    maxima, totals, blended = running
    result = (blended / totals[..., None]).reshape(rows_here, query_width).astype(jnp.bfloat16)
    return (result[None], new_storage[None])


def solution(mesh):
    return jax.shard_map(
        body,
        mesh=mesh,
        in_specs=(
            P("req", "blk", "tp"),
            P(),
            P("req", "tp"),
            P("tp"),
            P("req", None, "tp"),
            P(None, "tp"),
            P("req", None, "blk", None, "tp"),
            P("req"),
            P("req", None),
        ),
        out_specs=(P("req", "blk", "tp"), P("req", None, "blk", None, "tp")),
        check_vma=False,
    )
```

profile of v0, /device:TPU:35, one launch (start us, length us, event | category | flops | bytes accessed | tf_op | source)
XLA Modules:
  0.0 774.0 jit_solution(6554469855381495535)
XLA Ops:
  11.2 25.5 %all-gather.13.cloned.1.call-done = bf16[1,128,5120]{2,1,0:T(8,128)(2,1)} async-done(((bf16[1,128,1280]{2,1,0:T(8,128)(2,1)}), bf16[1,128,5120]{2,1,0:T(8,128)(2,1)}) %all-gather.13.cloned.1.call-update) | async-done | bytes 1310736 | tf_op jit(solution)/shard_map/all_gather | solution.py:68
  36.7 1.6 fusion.26
  38.4 59.7 %all-gather.9.cloned.1.call-done = bf16[5120,2,256]{2,1,0:T(2,128)(2,1)} async-done(((bf16[1280,2,256]{2,1,0:T(2,128)(2,1)}), bf16[5120,2,256]{2,1,0:T(2,128)(2,1)}) %all-gather.9.cloned.1.call-update) | async-done | bytes 5242896 | tf_op jit(solution)/shard_map/all_gather | solution.py:76
  98.1 3.5 copy.82
  106.3 60.9 %all-gather.15.cloned.1.call-done = bf16[2,2048,256]{2,1,0:T(8,128)(2,1)} async-done(((bf16[2,128,256]{2,1,0:T(8,128)(2,1)}), bf16[2,2048,256]{2,1,0:T(8,128)(2,1)}) %all-gather.15.cloned.1.call-update) | async-done | bytes 2097168 | tf_op jit(solution)/shard_map/all_gather | solution.py:105
  167.3 1.7 fusion.61
  168.9 1.1 reshape_squeeze.6
  170.7 3.5 fusion.40
  174.2 1.1 copy.66
  175.3 127.5 %all-gather.11.cloned.1.call-done = bf16[5120,1280]{1,0:T(8,128)(2,1)} async-done(((bf16[1280,1280]{1,0:T(8,128)(2,1)}), bf16[5120,1280]{1,0:T(8,128)(2,1)}) %all-gather.11.cloned.1.call-update) | async-done | bytes 13107216 | tf_op jit(solution)/shard_map/all_gather | solution.py:75
  302.8 6.6 convolution_add_fusion
  310.7 1.1 copy.59
  312.1 1.6 fusion.22
  313.7 2.1 fusion.21
  315.9 3.6 fusion.46
  319.4 299.3 %all-gather.17.cloned.1.call-done = bf16[1,2,112,128,256]{4,3,2,1,0:T(8,128)(2,1)} async-done(((bf16[1,2,7,128,256]{4,3,2,1,0:T(8,128)(2,1)}), bf16[1,2,112,128,256]{4,3,2,1,0:T(8,128)(2,1)}) %all-gather.17.cloned.1.call-update) | async-done | bytes 14680080 | tf_op jit(solution)/shard_map/all_gather | solution.py:141
  618.7 146.7 %while.17 = (s32[]{:T(128)}, f32[128,2,5]{0,2,1:T(8,128)S(1)}, f32[128,2,5]{0,2,1:T(8,128)S(1)}, f32[128,2,5,128]{0,3,2,1:T(8,128)}, pred[112]{0:T(512)(128)(4,1...) while((s32[]{:T(128)}, f32[128,2,5]{0,2,1:T(8,128)S(1)}, ...), condition=%wide.region_7.8_spmd, body=%wide.region_4.0_spmd.sunk | while | flops 343083520 | bytes 12208327 | solution.py:64
  618.9 1.1 constant_dynamic-slice_fusion.3
  621.2 2.7 fusion.76
  624.1 1.1 constant_dynamic-slice_fusion.3
  626.5 2.7 fusion.76
  629.3 1.1 constant_dynamic-slice_fusion.3
  631.7 2.7 fusion.76
  634.6 1.1 constant_dynamic-slice_fusion.3
  636.9 2.7 fusion.76
  639.8 1.1 constant_dynamic-slice_fusion.3
  642.2 2.7 fusion.76
  645.1 1.1 constant_dynamic-slice_fusion.3
  647.4 2.7 fusion.76
  650.3 1.1 constant_dynamic-slice_fusion.3
  652.7 2.7 fusion.76
  655.5 1.1 constant_dynamic-slice_fusion.3
  657.9 2.7 fusion.76
  660.8 1.1 constant_dynamic-slice_fusion.3
  663.1 2.7 fusion.76
  668.4 2.7 fusion.76
  671.3 1.1 constant_dynamic-slice_fusion.3
  673.6 2.7 fusion.76
  676.5 1.1 constant_dynamic-slice_fusion.3
  678.9 2.7 fusion.76
  681.7 1.1 constant_dynamic-slice_fusion.3
  684.1 2.7 fusion.76
  689.3 2.7 fusion.76
  692.2 1.1 constant_dynamic-slice_fusion.3
  694.6 2.7 fusion.76
  697.4 1.1 constant_dynamic-slice_fusion.3
  699.8 2.7 fusion.76
  705.0 2.7 fusion.76
  707.9 1.1 constant_dynamic-slice_fusion.3
  710.3 2.7 fusion.76
  713.2 1.1 constant_dynamic-slice_fusion.3
  715.5 2.7 fusion.76
  718.4 1.1 constant_dynamic-slice_fusion.3
  720.8 2.7 fusion.76
  726.0 2.7 fusion.76
  728.9 1.1 constant_dynamic-slice_fusion.3
  731.2 2.7 fusion.76
  736.5 2.7 fusion.76
  741.7 2.7 fusion.76
  746.9 2.7 fusion.76
  752.2 2.7 fusion.76
  757.4 2.7 fusion.76
  762.7 2.7 fusion.76
  765.4 1.1 divide_convert_fusion
  (313 shorter events, 61.1 us)
Async XLA Ops:
  7.2 29.5 %all-gather.13.cloned.1.call-start = ((), (), s32[]{:S(2)}) async-start(), calls=%async_computation.2 | async-start | bytes 1638400 | tf_op jit(solution)/shard_map/all_gather | solution.py:68
  7.9 90.2 %all-gather.9.cloned.1.call-start = ((), (), s32[]{:S(2)}) async-start(), calls=%async_computation | async-start | bytes 6553600 | tf_op jit(solution)/shard_map/all_gather | solution.py:76
  8.6 158.6 %all-gather.15.cloned.1.call-start = ((), (), s32[]{:S(2)}) async-start(), calls=%async_computation.3 | async-start | bytes 2228224 | tf_op jit(solution)/shard_map/all_gather | solution.py:105
  98.1 3.5 copy-start
  102.6 2.4 copy-start.3
  102.6 2.5 copy-start.4
  103.8 199.0 %all-gather.11.cloned.1.call-start = ((), (), s32[]{:S(2)}) async-start(), calls=%async_computation.1 | async-start | bytes 16384000 | tf_op jit(solution)/shard_map/all_gather | solution.py:75
  104.4 514.3 %all-gather.17.cloned.1.call-start = ((), (), s32[]{:S(2)}) async-start(), calls=%async_computation.4 | async-start | bytes 15597568 | tf_op jit(solution)/shard_map/all_gather | solution.py:141
  309.5 2.6 copy-start.2
  309.7 2.4 copy-start.1
Sparse Core Ops, SparseCore 0:
  9.8 26.8 all-gather.12
  38.5 59.5 all-gather.8
  104.0 63.2 all-gather.14
  168.9 133.8 all-gather.10
  304.5 314.2 all-gather.16
where the time goes:
time: 776 us; the launch traced here: 774 us
  waiting for transfers between devices  575 us (74%)
  matrix products  107 us (14%)
  local copies, waits for them, and re-layouts  48.8 us (6%)
  other arithmetic  26.9 us (3%)
  between operations  14.7 us (2%)
    all_gather x1, waiting for transfers between devices, body(): lax.all_gather(cache_storage, 'blk', axis=1, tiled=True)  299 us
    all_gather x1, waiting for transfers between devices, body(): lax.all_gather(w_query, 'req', axis=0, tiled=True)  127 us
    dot_general x29, matrix products, attend(): jnp.einsum('rgjk,kgd->rgjd', weights.astype(jnp.bfloat16), value_rows, pr...  79.7 us
    all_gather x1, waiting for transfers between devices, body(): every_page = lax.all_gather(fresh_pages, 'blk', axis=1, tiled=True)  60.9 us
    all_gather x1, waiting for transfers between devices, body(): lax.all_gather(w_keyval, 'req', axis=0, tiled=True)  59.7 us
    slice x28, local copies, waits for them, and re-layouts, advance(): segment[1].reshape(stride * PAGE_TOKENS, kv_heads_local, HEAD_SIZE)  29.8 us
    all_gather x1, waiting for transfers between devices, body(): whole = lax.all_gather(tokens[0], 'tp', axis=1, tiled=True)  25.5 us
    reduce_sum x29, other arithmetic, attend(): totals = totals * decays + jnp.sum(weights, axis=-1)  18.7 us
  transfers between devices with their start and end apart: 5, of which 5 were waited for; matrix products, arithmetic and copies ran while one was open for 4% of the time, Pallas kernels for 0%

commit v1 on v0

--- a/solution.py
+++ b/solution.py
@@ -65,16 +65,24 @@
 
 
 def body(tokens, gain, w_query, b_query, w_keyval, b_keyval, kv_cache, cached_pages, page_table):
+
+    def groups_obtain(block_here):
+        clean = lax.all_to_all(
+            jnp.stack([block_here] * lax.psum(1, axis_name="req")),
+            concat_axis=0,
+            axis_name="req",
+            split_axis=0,
+        )
+        taken_in = jnp.concatenate(clean, axis=0)
+        return taken_in
+
     whole = lax.all_gather(tokens[0], "tp", axis=1, tiled=True)
     normed = normalize(whole, gain)
     rows_here = normed.shape[0]
     query_width = w_query.shape[1]
     kv_width = w_keyval.shape[2]
     pair_width = 2 * kv_width
-    pieces = (
-        lax.all_gather(w_query, "req", axis=0, tiled=True),
-        lax.all_gather(w_keyval, "req", axis=0, tiled=True),
-    )
+    pieces = (groups_obtain(w_query), lax.all_gather(w_keyval, "req", axis=0, tiled=True))
     count = pieces[0].shape[0]
     query_sum = jnp.dot(normed, pieces[0], preferred_element_type=jnp.float32)
     pair_sum = jnp.dot(

time: 776 us -> 649 us (0.84)
  waiting for transfers between devices: 575 us -> 436 us
    all_to_all x0 -> x1, waiting for transfers between devices: none -> 142 us  [groups_obtain(): lax.all_to_all(jnp.stack([block_here] * lax.psum(1, axis_name='req')), co...]
    all_gather x1 -> x0, waiting for transfers between devices: 127 us -> none  [body(): lax.all_gather(w_query, 'req', axis=0, tiled=True)]
    all_gather x1, waiting for transfers between devices: 299 us -> 206 us  [body(): lax.all_gather(cache_storage, 'blk', axis=1, tiled=True)]
    all_gather x1, waiting for transfers between devices: 60.9 us -> 0.02 us  [body(): every_page = lax.all_gather(fresh_pages, 'blk', axis=1, tiled=True)]
  transfers between devices with their start and end apart: 5 -> 5, of which waited for: 5 -> 4; matrix products, arithmetic and copies ran while one was open for 4% -> 5% of each run, Pallas kernels for 0% -> 0%
where the time goes in v1:
time: 649 us; the launch traced here: 646 us
  waiting for transfers between devices  436 us (67%)
  matrix products  107 us (16%)
  local copies, waits for them, and re-layouts  54.3 us (8%)
  other arithmetic  26.2 us (4%)
  between operations  14.7 us (2%)
  starting transfers between devices  6.87 us (1%)
    all_gather x1, waiting for transfers between devices, body(): lax.all_gather(cache_storage, 'blk', axis=1, tiled=True)  206 us
    all_to_all x1, waiting for transfers between devices, groups_obtain(): lax.all_to_all(jnp.stack([block_here] * lax.psum(1, axis_name='req')), co...  142 us
    dot_general x29, matrix products, attend(): jnp.einsum('rgjk,kgd->rgjd', weights.astype(jnp.bfloat16), value_rows, pr...  80 us
    all_gather x1, waiting for transfers between devices, body(): lax.all_gather(w_keyval, 'req', axis=0, tiled=True)  59.7 us
    slice x28, local copies, waits for them, and re-layouts, advance(): segment[1].reshape(stride * PAGE_TOKENS, kv_heads_local, HEAD_SIZE)  29.8 us
    all_gather x1, waiting for transfers between devices, body(): whole = lax.all_gather(tokens[0], 'tp', axis=1, tiled=True)  25.6 us
    reduce_sum x29, other arithmetic, attend(): totals = totals * decays + jnp.sum(weights, axis=-1)  18.7 us
    dot_general x29, matrix products, attend(): jnp.einsum('rgjd,kgd->rgjk', query_rows_all, key_rows, preferred_element_...  16.1 us
  transfers between devices with their start and end apart: 5, of which 4 were waited for; matrix products, arithmetic and copies ran while one was open for 5% of the time, Pallas kernels for 0%

profile of v1, /device:TPU:35, one launch (start us, length us, event | category | flops | bytes accessed | tf_op | source)
XLA Modules:
  0.0 646.2 jit_solution(9154062852554492085)
XLA Ops:
  11.2 25.6 %all-gather.10.cloned.1.call-done = bf16[1,128,5120]{2,1,0:T(8,128)(2,1)} async-done(((bf16[1,128,1280]{2,1,0:T(8,128)(2,1)}), bf16[1,128,5120]{2,1,0:T(8,128)(2,1)}) %all-gather.10.cloned.1.call-update) | async-done | bytes 1310736 | tf_op jit(solution)/shard_map/all_gather | solution.py:79
  36.7 1.6 fusion.26
  38.4 59.7 %all-gather.8.cloned.1.call-done = bf16[5120,2,256]{2,1,0:T(2,128)(2,1)} async-done(((bf16[1280,2,256]{2,1,0:T(2,128)(2,1)}), bf16[5120,2,256]{2,1,0:T(2,128)(2,1)}) %all-gather.8.cloned.1.call-update) | async-done | bytes 5242896 | tf_op jit(solution)/shard_map/all_gather | solution.py:85
  98.1 3.5 copy.82
  104.4 7.2 %stack.15 = bf16[4,1280,1280]{2,1,0:T(8,128)(2,1)} broadcast(bf16[1280,1280]{1,0:T(8,128)(2,1)} %param.13), dimensions={1,2} | broadcast | bytes 16384000 | tf_op jit(solution)/shard_map/stack | solution.py:71
  111.6 6.7 %all-to-all-start = ((bf16[4,1280,1280]{2,1,0:T(8,128)(2,1)}), bf16[4,1280,1280]{2,1,0:T(8,128)(2,1)}, u32[]{:S(2)}, u32[]{:S(2)}) async-start(bf16[4,1280,1280]{2,1,0:T(8,128)(2,1)} %stack.15), calls=%async_computation | async-start | bytes 26214400 | tf_op jit(solution)/shard_map/all_to_all | solution.py:70
  119.7 142.3 %all-to-all-done = bf16[4,1280,1280]{2,1,0:T(8,128)(2,1)} async-done(((bf16[4,1280,1280]{2,1,0:T(8,128)(2,1)}), bf16[4,1280,1280]{2,1,0:T(8,128)(2,1)}, u32[]{:S(2)}, u32[]{:S(2)}) %all-to-all-start) | async-done | bytes 13107232 | tf_op jit(solution)/shard_map/all_to_all | solution.py:70
  261.9 6.7 %convolution_add_fusion = f32[128,1280]{1,0:T(8,128)S(1)} fusion(bf16[5120,1280]{1,0:T(8,128)(2,1)} %bitcast.10, bf16[1,128,5120]{2,1,0:T(8,128)(2,1)S(1)} %copy-done, f32[5120]{0:T(1024)S(1)} %convert_element_type.74, f32[128]{0:T(128)S(1)} %add_rsqrt_fusion, f32[1280]{0:T(1024)S(1)} %convert_element_type.80), kind=kOutput, calls=%fused_computation.35 | convolution fusion | flops 1680506880 | bytes 15099392 | tf_op jit(solution)/shard_map/dot_general | solution.py:87
  269.6 1.7 fusion.61
  272.3 3.5 fusion.40
  275.8 1.1 copy.66
  277.0 1.6 fusion.22
  278.6 2.1 fusion.21
  280.8 3.6 fusion.46
  284.3 206.1 %all-gather.14.cloned.1.call-done = bf16[1,2,112,128,256]{4,3,2,1,0:T(8,128)(2,1)} async-done(((bf16[1,2,7,128,256]{4,3,2,1,0:T(8,128)(2,1)}), bf16[1,2,112,128,256]{4,3,2,1,0:T(8,128)(2,1)}) %all-gather.14.cloned.1.call-update) | async-done | bytes 14680080 | tf_op jit(solution)/shard_map/all_gather | solution.py:149
  490.5 147.1 %while.17 = (s32[]{:T(128)}, f32[128,2,5]{0,2,1:T(8,128)S(1)}, f32[128,2,5]{0,2,1:T(8,128)S(1)}, f32[128,2,5,128]{0,3,2,1:T(8,128)}, pred[112]{0:T(512)(128)(4,1...) while((s32[]{:T(128)}, f32[128,2,5]{0,2,1:T(8,128)S(1)}, ...), condition=%wide.region_7.8_spmd, body=%wide.region_4.0_spmd.sunk | while | flops 343083520 | bytes 12208335 | solution.py:64
  490.6 1.1 constant_dynamic-slice_fusion.3
  493.0 2.7 fusion.76
  495.9 1.1 constant_dynamic-slice_fusion.3
  498.3 2.7 fusion.76
  501.1 1.1 constant_dynamic-slice_fusion.3
  503.5 2.7 fusion.76
  506.4 1.1 constant_dynamic-slice_fusion.3
  508.8 2.7 fusion.76
  511.7 1.1 constant_dynamic-slice_fusion.3
  514.0 2.7 fusion.76
  516.9 1.1 constant_dynamic-slice_fusion.3
  519.3 2.7 fusion.76
  522.2 1.1 constant_dynamic-slice_fusion.3
  524.5 2.7 fusion.76
  527.4 1.1 constant_dynamic-slice_fusion.3
  529.8 2.7 fusion.76
  532.7 1.1 constant_dynamic-slice_fusion.3
  535.0 2.7 fusion.76
  537.9 1.1 constant_dynamic-slice_fusion.3
  540.3 2.7 fusion.76
  545.6 2.7 fusion.76
  548.4 1.1 constant_dynamic-slice_fusion.3
  550.8 2.7 fusion.76
  553.7 1.1 constant_dynamic-slice_fusion.3
  556.1 2.7 fusion.76
  558.9 1.1 constant_dynamic-slice_fusion.3
  561.3 2.7 fusion.76
  564.2 1.1 constant_dynamic-slice_fusion.3
  566.6 2.7 fusion.76
  569.5 1.1 constant_dynamic-slice_fusion.3
  571.8 2.7 fusion.76
  577.1 2.7 fusion.76
  580.0 1.1 constant_dynamic-slice_fusion.3
  582.3 2.7 fusion.76
  585.2 1.1 constant_dynamic-slice_fusion.3
  587.6 2.7 fusion.76
  590.5 1.1 constant_dynamic-slice_fusion.3
  592.8 2.7 fusion.76
  595.7 1.1 constant_dynamic-slice_fusion.3
  598.1 2.7 fusion.76
  603.4 2.7 fusion.76
  608.6 2.7 fusion.76
  613.9 2.7 fusion.76
  619.1 2.7 fusion.76
  624.4 2.7 fusion.76
  629.6 2.7 fusion.76
  634.9 2.7 fusion.76
  637.6 1.1 divide_convert_fusion
  (311 shorter events, 59.3 us)
Async XLA Ops:
  7.2 29.5 %all-gather.10.cloned.1.call-start = ((), (), s32[]{:S(2)}) async-start(), calls=%async_computation.2 | async-start | bytes 1638400 | tf_op jit(solution)/shard_map/all_gather | solution.py:79
  7.9 90.2 %all-gather.8.cloned.1.call-start = ((), (), s32[]{:S(2)}) async-start(), calls=%async_computation.1 | async-start | bytes 6553600 | tf_op jit(solution)/shard_map/all_gather | solution.py:85
  8.6 261.0 %all-gather.12.cloned.1.call-start = ((), (), s32[]{:S(2)}) async-start(), calls=%async_computation.3 | async-start | bytes 2228224 | tf_op jit(solution)/shard_map/all_gather | solution.py:113
  98.1 3.5 copy-start
  103.8 386.7 %all-gather.14.cloned.1.call-start = ((), (), s32[]{:S(2)}) async-start(), calls=%async_computation.4 | async-start | bytes 15597568 | tf_op jit(solution)/shard_map/all_gather | solution.py:149
  111.6 6.7 %copy-start.2 = (bf16[1280]{0:T(1024)(128)(2,1)S(1)}, bf16[1280]{0:T(1024)(128)(2,1)}, u32[]{:S(2)}) copy-start(bf16[1280]{0:T(1024)(128)(2,1)} %param.14) | copy-start | bytes 7684
  111.6 6.8 %copy-start.3 = (s32[1,80]{1,0:T(1,128)S(1)}, s32[1,80]{1,0:T(1,128)}, u32[]{:S(2)}) copy-start(s32[1,80]{1,0:T(1,128)} %param.19) | copy-start | bytes 964
  111.6 150.3 %all-to-all-start = ((bf16[4,1280,1280]{2,1,0:T(8,128)(2,1)}), bf16[4,1280,1280]{2,1,0:T(8,128)(2,1)}, u32[]{:S(2)}, u32[]{:S(2)}) async-start(bf16[4,1280,1280]{2,1,0:T(8,128)(2,1)} %stack.15), calls=%async_computation | async-start | bytes 26214400 | tf_op jit(solution)/shard_map/all_to_all | solution.py:70
  272.3 4.7 copy-start.1
Sparse Core Ops, SparseCore 0:
  9.8 26.8 all-gather.9
  38.5 59.5 all-gather.7
  103.9 63.2 all-gather.11
  168.9 321.5 all-gather.13
